TPU v7x, 32 devices: a whole 2x2x4 slice. The times are simulated.
32 devices in a mesh: gx: 2 (over core), gy: 4 (over y, x), gz: 4 (over z).
Axes of the slice: x: 2, y: 2, z: 4, core: 2. Of those that a mesh axis runs over, the one named last changes fastest.
Arguments:
- jacobian: bfloat16 [1024, 7, 135, 135], P(('gx', 'gy', 'gz')), may hold values from -6 to 6
- prolong: bfloat16 [1024, 135, 135], P(('gx', 'gy', 'gz')), may hold values from -0.5 to 0.5
- residual: bfloat16 [1024, 135], P(('gx', 'gy', 'gz')), may hold values from -6 to 6
- neighbours: int32 [1024, 6], P(('gx', 'gy', 'gz')), may hold values from -1 to 1023, as said below
- agg_map: int32 [1024], P(('gx', 'gy', 'gz')), may hold values from 0 to 127, as said below
- owners: int32 [128], P(('gx', 'gy', 'gz')), may hold values from 0 to 3, as said below
Outputs:
- coarse: bfloat16 [128, 7, 135, 135], P(('gx', 'gy', 'gz'))
- restricted: bfloat16 [128, 135], P(('gx', 'gy', 'gz'))
Inputs may be any that keep to these rules, and one draw needn't show every extreme that they name: `neighbours`: elements form a structured grid of bricks of 4 x 4 x 2 per device, laid out by the device's gx, gy, gz index; inside a device their numbering is an arbitrary permutation. The neighbour in direction -x or +x lies on the same device or on the device one step along gx (likewise y with gy, z with gz); exactly 8, 8 and 16 elements of a device have their x, y and z neighbour of one side off the device or absent. `agg_map`: aggregates are cubes of 2 x 2 x 2 elements of one device's brick; device d holds aggregates d * 4 to (d + 1) * 4 - 1. `owners`: owners are multiples of 1; each device hands exactly 1 of its aggregates to each such owner.
All inputs are finite; a program needn't handle non-finite values.
Results may differ from a plain program's by a relative error of at most 0.0051.
Values may be sent and summed in bfloat16 or wider, within the bound.
A program may use at most 192 MiB of HBM per device.

v0:
```python
import jax
import jax.numpy as jnp
from jax import lax
from jax.sharding import PartitionSpec as P

LX = 4
LY = 4
LZ = 2


def from_behind(value, axis, steps):
    count = lax.axis_size(axis)
    initial, last = (max(0, -steps), min(count, count - steps))
    return lax.ppermute(value, axis, [(source, source + steps) for source in range(initial, last)])


def fetch_faces(blocks, axis_num, offset):
    if axis_num == 0:
        return from_behind(blocks, "gx", offset)
    if axis_num == 1:
        return from_behind(blocks, "gy", offset)
    return from_behind(blocks, "gz", offset)


def body(jacobian, prolong, residual, neighbours, agg_map, owners):
    elems = jacobian.shape[0]
    width = prolong.shape[1]
    aggs_here = owners.shape[0]
    size_y = lax.axis_size("gy")
    size_z = lax.axis_size("gz")
    per_owner = aggs_here // 4
    device = (lax.axis_index("gx") * size_y + lax.axis_index("gy")) * size_z + lax.axis_index("gz")
    id_base = device * elems
    local_ids = neighbours - id_base
    on_device = (local_ids >= 0) & (local_ids < elems)
    is_valid = neighbours >= 0
    off_device = is_valid & jnp.logical_not(on_device)
    strides = (size_y * size_z, size_z, 1)
    face_sizes = (LY * LZ, LX * LZ, LX * LY)
    flat_blocks = prolong.reshape(elems, width * width)
    elem_counter = jnp.arange(elems, dtype=jnp.int32)
    pool_parts = [flat_blocks]
    columns = [elem_counter]
    live = [jnp.ones((elems,), bool)]
    pool_start = elems
    for direction in range(6):
        axis_num = direction // 2
        offset = 1 if direction % 2 == 0 else -1
        source_base = id_base - offset * strides[axis_num] * elems
        source_ids = neighbours[:, direction] - source_base
        face_count = face_sizes[axis_num]
        opposite = direction ^ 1
        on_face = jnp.logical_not(on_device[:, opposite])
        face_rank = jnp.cumsum(on_face.astype(jnp.int32)) - 1
        pack_select = (
            (jnp.arange(face_count, dtype=jnp.int32)[:, None] == face_rank[None, :])
            & on_face[None, :]
        ).astype(jnp.bfloat16)
        packed = jnp.dot(pack_select, flat_blocks, preferred_element_type=jnp.float32).astype(
            jnp.bfloat16
        )
        fetched = fetch_faces(packed, axis_num, offset)
        lower = off_device[None, :, direction] & (source_ids[None, :] < source_ids[:, None])
        position = jnp.sum(lower.astype(jnp.int32), axis=1)
        far_column = pool_start + position
        pool_start = pool_start + face_count
        pool_parts.append(fetched)
        columns.append(jnp.where(on_device[:, direction], local_ids[:, direction], far_column))
        live.append(is_valid[:, direction])
    pool = jnp.concatenate(pool_parts, axis=0)
    column_ids = jnp.stack(columns, axis=1)
    live_pairs = jnp.stack(live, axis=1)
    pick = (
        (column_ids[:, :, None] == jnp.arange(pool_start, dtype=jnp.int32)[None, None, :])
        & live_pairs[:, :, None]
    ).astype(jnp.bfloat16)
    gathered = jnp.einsum("edt,tx->edx", pick, pool, preferred_element_type=jnp.float32).astype(
        jnp.bfloat16
    )
    gathered = gathered.reshape(elems, 7, width, width)
    products = jnp.einsum(
        "edij,edjk->edik", jacobian, gathered, preferred_element_type=jnp.float32
    ).astype(jnp.bfloat16)
    triple = jnp.einsum("eji,edjk->edik", prolong, products, preferred_element_type=jnp.float32)
    near_agg = agg_map[jnp.clip(local_ids, 0, elems - 1)]
    same_agg = on_device & (near_agg == agg_map[:, None])
    slot_ids = jnp.where(same_agg, 0, jnp.arange(1, 7, dtype=jnp.int32)[None, :])
    slot_ids = jnp.concatenate([jnp.zeros((elems, 1), jnp.int32), slot_ids], axis=1)
    present = jnp.concatenate([jnp.ones((elems, 1), bool), is_valid], axis=1)
    slot_hot = (
        (slot_ids[:, :, None] == jnp.arange(7, dtype=jnp.int32)) & present[:, :, None]
    ).astype(jnp.float32)
    agg_hot = (
        (agg_map - device * aggs_here)[:, None] == jnp.arange(aggs_here, dtype=jnp.int32)
    ).astype(jnp.float32)
    coarse_rows = jnp.einsum(
        "ea,eds,edik->asik", agg_hot, slot_hot, triple, precision=lax.Precision.HIGHEST
    ).astype(jnp.bfloat16)
    per_element = jnp.einsum("eji,ej->ei", prolong, residual, preferred_element_type=jnp.float32)
    restr = jnp.dot(agg_hot.T, per_element, precision=lax.Precision.HIGHEST).astype(jnp.bfloat16)
    agg_counter = jnp.arange(aggs_here, dtype=jnp.int32)
    earlier = (owners[None, :] == owners[:, None]) & (agg_counter[None, :] < agg_counter[:, None])
    within = jnp.sum(earlier.astype(jnp.int32), axis=1)
    send_slot = owners * per_owner + within
    select = (
        jnp.arange(size_z * per_owner, dtype=jnp.int32)[:, None] == send_slot[None, :]
    ).astype(jnp.bfloat16)
    send_rows = jnp.einsum(
        "pa,asik->psik", select, coarse_rows, preferred_element_type=jnp.float32
    ).astype(jnp.bfloat16)
    send_restr = jnp.dot(select, restr, preferred_element_type=jnp.float32).astype(jnp.bfloat16)
    received = (
        lax.all_to_all(send_rows, "gz", split_axis=0, concat_axis=0, tiled=True),
        lax.all_to_all(send_restr, "gz", split_axis=0, concat_axis=0, tiled=True),
    )
    return (received[0], received[1])


def solution(mesh):
    return jax.shard_map(
        body,
        mesh=mesh,
        in_specs=(
            P(("gx", "gy", "gz"), None, None, None),
            P(("gx", "gy", "gz"), None, None),
            P(("gx", "gy", "gz"), None),
            P(("gx", "gy", "gz"), None),
            P(("gx", "gy", "gz")),
            P(("gx", "gy", "gz")),
        ),
        out_specs=(P(("gx", "gy", "gz"), None, None, None), P(("gx", "gy", "gz"), None)),
        check_vma=False,
    )
```

profile of v0, /device:TPU:0, one launch (start us, length us, event | category | flops | bytes accessed | tf_op | source)
XLA Modules:
  0.0 275.0 jit_solution(7377247177261924681)
XLA Ops:
  0.7 0.7 compare_select_fusion
  1.4 0.1 copy.76
  1.5 0.1 reshape.299
  1.6 1.6 gather_fusion
  3.2 0.1 reshape.298
  3.3 0.1 copy.77
  3.4 0.1 copy.67
  3.6 0.1 add_reduce_fusion.5
  3.7 2.7 copy.66
  6.4 3.4 %reshape.295 = bf16[32,18225]{1,0:T(8,128)(2,1)S(1)} reshape(bf16[32,135,135]{2,1,0:T(8,128)(2,1)} %copy.66) | data formatting | bytes 2332800 | tf_op jit(solution)/shard_map/reshape | solution.py:40
  9.7 1.0 convolution_convert_fusion.6
  10.7 3.2 %collective-permute-start = (bf16[8,18225]{1,0:T(8,128)(2,1)}, bf16[8,18225]{1,0:T(8,128)(2,1)}, u32[]{:S(2)}, u32[]{:S(2)}) collective-permute-start(bf16[8,18225]{1,0:T(8,128)(2,1)} %convolution_convert_fusion.6), channel_id=1, source_target_pairs={{0,16},{1,17},{2,18},{3,19},{4,20},{5,21},{6,22},{7,23},{8,24},{9,... | collective-permute-start | bytes 874808 | tf_op jit(solution)/shard_map/ppermute | solution.py:14
  14.0 0.1 copy.68
  14.1 0.1 add_reduce_fusion.4
  14.2 1.0 convolution_convert_fusion.5
  15.2 1.3 collective-permute-start.1
  16.5 0.1 copy.69
  16.6 0.1 add_reduce_fusion.3
  16.7 1.0 convolution_convert_fusion.4
  17.7 4.9 %collective-permute-start.2 = (bf16[8,18225]{1,0:T(8,128)(2,1)}, bf16[8,18225]{1,0:T(8,128)(2,1)}, u32[]{:S(2)}, u32[]{:S(2)}) collective-permute-start(bf16[8,18225]{1,0:T(8,128)(2,1)} %convolution_convert_fusion.4), channel_id=1, source_target_pairs={{0,4},{4,8},{8,12},{1,5},{5,9},{9,13},{2,6},{6,10},{10,14},{3,7},{... | collective-permute-start | bytes 874808 | tf_op jit(solution)/shard_map/ppermute | solution.py:14
  22.7 0.1 copy.70
  22.8 0.1 add_reduce_fusion.2
  22.9 1.0 convolution_convert_fusion.3
  23.9 1.3 collective-permute-start.3
  25.2 0.1 copy.71
  25.4 0.1 add_reduce_fusion.1
  25.5 1.1 convolution_convert_fusion.2
  26.6 4.3 %collective-permute-start.4 = (bf16[16,18225]{1,0:T(8,128)(2,1)}, bf16[16,18225]{1,0:T(8,128)(2,1)}, u32[]{:S(2)}, u32[]{:S(2)}) collective-permute-start(bf16[16,18225]{1,0:T(8,128)(2,1)} %convolution_convert_fusion.2), channel_id=1, source_target_pairs={{0,1},{1,2},{2,3},{4,5},{5,6},{6,7},{8,9},{9,10},{10,11},{12,13},{... | collective-permute-start | bytes 1749608 | tf_op jit(solution)/shard_map/ppermute | solution.py:14
  30.9 0.2 convert_reduce_fusion.6
  31.1 1.3 fusion.40
  32.4 0.1 convolution_convert_fusion.8
  32.5 0.1 fusion.27
  32.6 0.6 copy.83
  33.2 3.2 %all-to-all-start.1 = ((bf16[4,1,135]{2,1,0:T(2,128)(2,1)}), bf16[4,1,135]{2,1,0:T(2,128)(2,1)S(1)}, u32[]{:S(2)}, u32[]{:S(2)}) async-start(bf16[4,1,135]{2,1,0:T(2,128)(2,1)} %copy.83), calls=%async_computation.1 | async-start | bytes 8192 | tf_op jit(solution)/shard_map/all_to_all | solution.py:114
  36.5 1.1 constant_dynamic-update-slice_fusion.6
  37.6 0.1 copy.72
  37.8 0.2 convert_reduce_fusion
  37.9 0.2 convert_reduce_fusion.2
  38.1 0.2 convert_reduce_fusion.4
  38.3 0.1 add_reduce_fusion
  38.5 0.1 copy.79
  38.6 0.1 copy.96
  38.7 0.1 concatenate.8.clone
  38.8 0.3 convolution_convert_fusion.1
  39.1 1.3 collective-permute-start.5
  40.4 1.7 constant_dynamic-update-slice_fusion.5
  42.1 1.7 constant_dynamic-update-slice_fusion.4
  43.8 1.7 constant_dynamic-update-slice_fusion.3
  45.5 1.7 constant_dynamic-update-slice_fusion.2
  47.2 1.9 constant_dynamic-update-slice_fusion.1
  49.1 7.7 %collective-permute-done.5 = bf16[16,18225]{1,0:T(8,128)(2,1)S(1)} collective-permute-done((bf16[16,18225]{1,0:T(8,128)(2,1)S(1)}, bf16[16,18225]{1,0:T(8,128)(2,1)S(1)}, u32[]{:S(2)}, u32[]{:S(2)}) %collective-permute-start.5) | collective-permute-done | bytes 583232 | tf_op jit(solution)/shard_map/ppermute | solution.py:14
  56.8 0.9 constant_dynamic-update-slice_fusion
  57.6 7.6 %convolution_convert_fusion = bf16[32,7,18225]{2,0,1:T(8,128)(2,1)} fusion(bf16[96,18225]{1,0:T(8,128)(2,1)} %constant_dynamic-update-slice_fusion, s32[32,7]{0,1:T(8,128)S(1)} %stack.5, pred[32,7]{0,1:T(8,128)(4,1)S(1)} %stack.6), kind=kOutput, calls=%fused_computation.3 | convolution fusion | flops 787946240 | bytes 11665120 | tf_op jit(solution)/shard_map/edt,tx->edx/dot_general | solution.py:77
  65.2 21.7 %reshape.296 = bf16[32,7,135,135]{3,2,0,1:T(8,128)(2,1)} reshape(bf16[32,7,18225]{2,0,1:T(8,128)(2,1)} %convolution_convert_fusion) | data formatting | bytes 16329600 | tf_op jit(solution)/shard_map/reshape | solution.py:80
  86.9 27.6 %fusion.8 = f32[32,7,135,135]{2,3,1,0:T(8,128)} fusion(bf16[32,7,135,135]{3,2,0,1:T(8,128)(2,1)} %reshape.296, bf16[32,7,135,135]{3,0,2,1:T(8,128)(2,1)} %param.6, bf16[32,135,135,1]{2,0,1,3:T(8,128)(2,1)S(1)} %bitcast.97), kind=kOutput, calls=%fused_computation.16 | convolution fusion | flops 2208578304 | bytes 33825600 | tf_op jit(solution)/shard_map/eji,edjk->edik/dot_general | solution.py:84
  114.5 38.7 %copy.80 = f32[32,7,135,135]{3,1,2,0:T(8,128)} copy(f32[32,7,135,135]{2,3,1,0:T(8,128)} %fusion.8) | data formatting | bytes 32659200 | tf_op jit(solution)/shard_map/eji,edjk->edik/transpose | solution.py:84
  153.2 32.7 %fusion.30 = f32[32,135,135,7]{2,3,1,0:T(8,128)} fusion(f32[32,7,135,135]{3,1,2,0:T(8,128)} %copy.80, s32[32,7]{1,0:T(8,128)S(1)} %concatenate.8.clone, pred[32,7]{1,0:T(8,128)(4,1)S(1)} %copy.79), kind=kOutput, calls=%fused_computation.29 | convolution fusion | flops 342924736 | bytes 32660320 | tf_op jit(solution)/shard_map/ea,eds,edik->asik/dot_general | solution.py:96
  185.9 34.6 %fusion = bf16[135,135,7,4]{1,3,0,2:T(4,128)(2,1)S(1)} fusion(f32[32,135,135,7]{2,3,1,0:T(8,128)} %fusion.30, s32[32]{0:T(128)S(1)} %broadcast_subtract_fusion.1), kind=kOutput, calls=%fused_computation.1 | convolution fusion | flops 195955328 | bytes 17350328 | tf_op jit(solution)/shard_map/ea,eds,edik->asik/dot_general | solution.py:96
  220.5 1.1 fusion.24
  221.7 1.5 copy.82
  223.2 4.4 %all-to-all-start = ((bf16[4,7,135,135]{3,2,1,0:T(8,128)(2,1)}), bf16[4,7,135,135]{3,2,1,0:T(8,128)(2,1)S(1)}, u32[]{:S(2)}, u32[]{:S(2)}) async-start(bf16[4,7,135,135]{3,2,1,0:T(8,128)(2,1)} %copy.82), calls=%async_computation | async-start | bytes 3899392 | tf_op jit(solution)/shard_map/all_to_all | solution.py:113
  227.7 0.6 copy.122
  228.3 44.7 %all-to-all-done = bf16[4,7,135,135]{3,2,1,0:T(8,128)(2,1)S(1)} async-done(((bf16[4,7,135,135]{3,2,1,0:T(8,128)(2,1)}), bf16[4,7,135,135]{3,2,1,0:T(8,128)(2,1)S(1)}, u32[]{:S(2)}, u32[]{:S(2)}) %all-to-all-start) | async-done | bytes 1020632 | tf_op jit(solution)/shard_map/all_to_all | solution.py:113
  273.0 2.0 copy.84
  (37 shorter events, 0.6 us)
Async XLA Ops:
  0.6 30.5 %copy-start = (bf16[32,135]{1,0:T(8,128)(2,1)S(1)}, bf16[32,135]{1,0:T(8,128)(2,1)}, u32[]{:S(2)}) copy-start(bf16[32,135]{1,0:T(8,128)(2,1)} %param.8) | copy-start | bytes 25924
  0.6 0.9 copy-start.2
  1.6 2.1 copy-start.3
  10.7 20.2 %copy-start.5 = (s32[4]{0:T(128)S(1)}, s32[4]{0:T(128)}, u32[]{:S(2)}) copy-start(s32[4]{0:T(128)} %param.11) | copy-start | bytes 52
  10.7 28.4 %collective-permute-start = (bf16[8,18225]{1,0:T(8,128)(2,1)}, bf16[8,18225]{1,0:T(8,128)(2,1)}, u32[]{:S(2)}, u32[]{:S(2)}) collective-permute-start(bf16[8,18225]{1,0:T(8,128)(2,1)} %convolution_convert_fusion.6), channel_id=1, source_target_pairs={{0,16},{1,17},{2,18},{3,19},{4,20},{5,21},{6,22},{7,23},{8,24},{9,... | collective-permute-start | bytes 874808 | tf_op jit(solution)/shard_map/ppermute | solution.py:14
  15.2 26.9 %collective-permute-start.1 = (bf16[8,18225]{1,0:T(8,128)(2,1)}, bf16[8,18225]{1,0:T(8,128)(2,1)}, u32[]{:S(2)}, u32[]{:S(2)}) collective-permute-start(bf16[8,18225]{1,0:T(8,128)(2,1)} %convolution_convert_fusion.5), channel_id=1, source_target_pairs={{16,0},{17,1},{18,2},{19,3},{20,4},{21,5},{22,6},{23,7},{24,8},{25... | collective-permute-start | bytes 874808 | tf_op jit(solution)/shard_map/ppermute | solution.py:14
  17.7 26.0 %collective-permute-start.2 = (bf16[8,18225]{1,0:T(8,128)(2,1)}, bf16[8,18225]{1,0:T(8,128)(2,1)}, u32[]{:S(2)}, u32[]{:S(2)}) collective-permute-start(bf16[8,18225]{1,0:T(8,128)(2,1)} %convolution_convert_fusion.4), channel_id=1, source_target_pairs={{0,4},{4,8},{8,12},{1,5},{5,9},{9,13},{2,6},{6,10},{10,14},{3,7},{... | collective-permute-start | bytes 874808 | tf_op jit(solution)/shard_map/ppermute | solution.py:14
  23.9 21.6 %collective-permute-start.3 = (bf16[8,18225]{1,0:T(8,128)(2,1)}, bf16[8,18225]{1,0:T(8,128)(2,1)}, u32[]{:S(2)}, u32[]{:S(2)}) collective-permute-start(bf16[8,18225]{1,0:T(8,128)(2,1)} %convolution_convert_fusion.3), channel_id=1, source_target_pairs={{4,0},{8,4},{12,8},{5,1},{9,5},{13,9},{6,2},{10,6},{14,10},{7,3},{... | collective-permute-start | bytes 874808 | tf_op jit(solution)/shard_map/ppermute | solution.py:14
  25.5 12.1 %copy-start.4 = (s32[32,6]{0,1:T(8,128)S(1)}, s32[32,6]{0,1:T(8,128)}, u32[]{:S(2)}) copy-start(s32[32,6]{0,1:T(8,128)} %param.9) | copy-start | bytes 2308
  26.6 20.6 %collective-permute-start.4 = (bf16[16,18225]{1,0:T(8,128)(2,1)}, bf16[16,18225]{1,0:T(8,128)(2,1)}, u32[]{:S(2)}, u32[]{:S(2)}) collective-permute-start(bf16[16,18225]{1,0:T(8,128)(2,1)} %convolution_convert_fusion.2), channel_id=1, source_target_pairs={{0,1},{1,2},{2,3},{4,5},{5,6},{6,7},{8,9},{9,10},{10,11},{12,13},{... | collective-permute-start | bytes 1749608 | tf_op jit(solution)/shard_map/ppermute | solution.py:14
  33.2 190.0 %all-to-all-start.1 = ((bf16[4,1,135]{2,1,0:T(2,128)(2,1)}), bf16[4,1,135]{2,1,0:T(2,128)(2,1)S(1)}, u32[]{:S(2)}, u32[]{:S(2)}) async-start(bf16[4,1,135]{2,1,0:T(2,128)(2,1)} %copy.83), calls=%async_computation.1 | async-start | bytes 8192 | tf_op jit(solution)/shard_map/all_to_all | solution.py:114
  39.1 17.7 %collective-permute-start.5 = (bf16[16,18225]{1,0:T(8,128)(2,1)S(1)}, bf16[16,18225]{1,0:T(8,128)(2,1)S(1)}, u32[]{:S(2)}, u32[]{:S(2)}) collective-permute-start(bf16[16,18225]{1,0:T(8,128)(2,1)S(1)} %convolution_convert_fusion.1), channel_id=1, source_target_pairs={{1,0},{2,1},{3,2},{5,4},{6,5},{7,6},{9,8},{10,9},{11,10},{13,12},{... | collective-permute-start | bytes 1749608 | tf_op jit(solution)/shard_map/ppermute | solution.py:14
  221.7 53.3 %copy-start.1 = (bf16[32,135]{1,0:T(8,128)(2,1)S(1)}, bf16[32,135]{1,0:T(8,128)(2,1)}, u32[]{:S(2)}) copy-start(bf16[32,135]{1,0:T(8,128)(2,1)} %param.8) | copy-start | bytes 25924
  223.2 49.8 %all-to-all-start = ((bf16[4,7,135,135]{3,2,1,0:T(8,128)(2,1)}), bf16[4,7,135,135]{3,2,1,0:T(8,128)(2,1)S(1)}, u32[]{:S(2)}, u32[]{:S(2)}) async-start(bf16[4,7,135,135]{3,2,1,0:T(8,128)(2,1)} %copy.82), calls=%async_computation | async-start | bytes 3899392 | tf_op jit(solution)/shard_map/all_to_all | solution.py:113
where the time goes:
time: 277 us; the launch traced here: 275 us
  matrix products  111 us (40%)
  local copies, waits for them, and re-layouts  84.6 us (31%)
  waiting for transfers between devices  52.4 us (19%)
  starting transfers between devices  24 us (9%)
    dot_general x2, matrix products, body(): jnp.einsum('ea,eds,edik->asik', agg_hot, slot_hot, triple, precision=lax....  67.3 us
    all_to_all x1, waiting for transfers between devices, body(): lax.all_to_all(send_rows, 'gz', split_axis=0, concat_axis=0, tiled=True)  44.7 us
    transpose x1, local copies, waits for them, and re-layouts, body(): jnp.einsum('eji,edjk->edik', prolong, products, preferred_element_type=jn...  38.7 us
    dot_general x1, matrix products, body(): jnp.einsum('eji,edjk->edik', prolong, products, preferred_element_type=jn...  27.6 us
    reshape x1, local copies, waits for them, and re-layouts, body(): gathered = gathered.reshape(elems, 7, width, width)  21.7 us
    ppermute x6, starting transfers between devices, from_behind(): lax.ppermute(value, axis, [(source, source + steps) for source in range(i...  16.3 us
    unnamed x22, local copies, waits for them, and re-layouts  15.2 us
    ppermute x6, waiting for transfers between devices, from_behind(): lax.ppermute(value, axis, [(source, source + steps) for source in range(i...  7.67 us
  transfers between devices with their start and end apart: 8, of which 2 were waited for; matrix products, arithmetic and copies ran while one was open for 68% of the time, Pallas kernels for 0%

commit v1 on v0

v1 whole, which is shorter than its diff:
```python
import jax
import jax.numpy as jnp
from jax import lax
from jax.experimental import pallas as pl
from jax.experimental.pallas import tpu as pltpu
from jax.sharding import PartitionSpec as P

LX = 4
LY = 4
LZ = 2


def from_behind(value, axis, steps):
    count = lax.axis_size(axis)
    initial, last = (max(0, -steps), min(count, count - steps))
    return lax.ppermute(value, axis, [(source, source + steps) for source in range(initial, last)])


def fetch_faces(blocks, axis_num, offset):
    if axis_num == 0:
        return from_behind(blocks, "gx", offset)
    if axis_num == 1:
        return from_behind(blocks, "gy", offset)
    return from_behind(blocks, "gz", offset)


def coarse_kernel(columns, slots, aggs, dest, prolong, faces, jacobian, out_slots, aggs_here):
    elems, width, _ = prolong.shape
    head = width // 128 * 128
    rest = width - head
    zero_block = elems + max(face.shape[0] for face in faces)
    step_rows = 5 if width % 5 == 0 else 1

    def kernel(col_ref, slot_ref, agg_ref, dest_ref, p_ref, *refs):
        face_refs = refs[:6]
        j_ref, head_ref, tail_ref, pool, flipped, near, far, total = refs[6:]
        k = pl.program_id(0)

        @pl.when(k == 0)
        def _():
            total[...] = jnp.zeros_like(total)
            head_ref[...] = jnp.zeros_like(head_ref)
            tail_ref[...] = jnp.zeros_like(tail_ref)
            pool[zero_block] = jnp.zeros((width, width), pool.dtype)

            @pl.loop(0, elems)
            def _(e):
                pool[e] = p_ref[e]
                flipped[e] = p_ref[e].astype(jnp.float32).T.astype(flipped.dtype)

        for d, face_ref in enumerate(face_refs):

            @pl.when(k == d + 1)
            def _(face_ref=face_ref):
                @pl.loop(0, face_ref.shape[0])
                def _(n):
                    pool[elems + n] = face_ref[n]

        @pl.loop(0, width // step_rows)
        def _(c):
            part = j_ref[0, pl.ds(c * step_rows, step_rows)].astype(jnp.float32)
            part = part.reshape(step_rows * elems, width)
            rows = pl.ds(pl.multiple_of(c * step_rows * elems, 8), step_rows * elems)
            near[rows, :] = part[:, :head]
            far[rows, :rest] = part[:, head:]

        @pl.loop(0, elems // 4)
        def _(group):
            for u in range(4):
                e = group * 4 + u
                own = jnp.concatenate(
                    [
                        near[pl.ds(e, width, stride=elems), :],
                        far[pl.ds(e, width, stride=elems), :],
                    ],
                    axis=1,
                )[:, :width].astype(jnp.bfloat16)
                product = jnp.dot(
                    own, pool[col_ref[e * 7 + k]], preferred_element_type=jnp.float32
                ).astype(jnp.bfloat16)
                triple = jnp.dot(flipped[e], product, preferred_element_type=jnp.float32)
                total[agg_ref[e], slot_ref[e * 7 + k]] += triple

        @pl.when(k == 6)
        def _():
            @pl.loop(0, aggs_here)
            def _(a):
                to = dest_ref[a]
                for s in range(7):
                    row = total[a, s]
                    head_ref[to, s] = row[:, :head].astype(jnp.bfloat16)
                    tail_ref[to, :, s * rest : (s + 1) * rest] = row[:, head:].astype(jnp.bfloat16)

    whole = pl.BlockSpec(memory_space=pltpu.VMEM)
    return pl.pallas_call(
        kernel,
        grid_spec=pltpu.PrefetchScalarGridSpec(
            num_scalar_prefetch=4,
            grid=(7,),
            in_specs=[whole] * 7
            + [pl.BlockSpec((1, width, elems, width), lambda k, *_: (k, 0, 0, 0))],
            out_specs=[whole, whole],
            scratch_shapes=[
                pltpu.VMEM((zero_block + 1, width, width), jnp.bfloat16),
                pltpu.VMEM((elems, width, width), jnp.bfloat16),
                pltpu.VMEM((width * elems, head), jnp.float32),
                pltpu.VMEM((width * elems, 128), jnp.float32),
                pltpu.VMEM((aggs_here, 7, width, width), jnp.float32),
            ],
        ),
        out_shape=[
            jax.ShapeDtypeStruct((out_slots, 7, width, head), jnp.bfloat16),
            jax.ShapeDtypeStruct((out_slots, width, pl.cdiv(7 * rest, 128) * 128), jnp.bfloat16),
        ],
        compiler_params=pltpu.CompilerParams(vmem_limit_bytes=56 << 20),
    )(columns, slots, aggs, dest, prolong, *faces, jnp.transpose(jacobian, (1, 2, 0, 3)))


def body(jacobian, prolong, residual, neighbours, agg_map, owners):
    elems = jacobian.shape[0]
    width = prolong.shape[1]
    aggs_here = owners.shape[0]
    size_y = lax.axis_size("gy")
    size_z = lax.axis_size("gz")
    per_owner = aggs_here // 4
    device = (lax.axis_index("gx") * size_y + lax.axis_index("gy")) * size_z + lax.axis_index("gz")
    id_base = device * elems
    local_ids = neighbours - id_base
    on_device = (local_ids >= 0) & (local_ids < elems)
    is_valid = neighbours >= 0
    off_device = is_valid & jnp.logical_not(on_device)
    zero_block = elems + max(LY * LZ, LX * LZ, LX * LY)
    strides = (size_y * size_z, size_z, 1)
    face_sizes = (LY * LZ, LX * LZ, LX * LY)
    flat_blocks = prolong.reshape(elems, width * width)
    elem_counter = jnp.arange(elems, dtype=jnp.int32)
    faces = []
    columns = [elem_counter]
    for direction in range(6):
        axis_num = direction // 2
        offset = 1 if direction % 2 == 0 else -1
        source_base = id_base - offset * strides[axis_num] * elems
        source_ids = neighbours[:, direction] - source_base
        face_count = face_sizes[axis_num]
        opposite = direction ^ 1
        on_face = jnp.logical_not(on_device[:, opposite])
        face_rank = jnp.cumsum(on_face.astype(jnp.int32)) - 1
        pack_select = (
            (jnp.arange(face_count, dtype=jnp.int32)[:, None] == face_rank[None, :])
            & on_face[None, :]
        ).astype(jnp.bfloat16)
        packed = jnp.dot(pack_select, flat_blocks, preferred_element_type=jnp.float32).astype(
            jnp.bfloat16
        )
        fetched = fetch_faces(packed, axis_num, offset)
        lower = off_device[None, :, direction] & (source_ids[None, :] < source_ids[:, None])
        position = jnp.sum(lower.astype(jnp.int32), axis=1)
        far_column = elems + position
        faces.append(fetched.reshape(face_count, width, width))
        near_column = jnp.where(on_device[:, direction], local_ids[:, direction], far_column)
        columns.append(jnp.where(is_valid[:, direction], near_column, zero_block))
    near_agg = agg_map[jnp.clip(local_ids, 0, elems - 1)]
    same_agg = on_device & (near_agg == agg_map[:, None])
    slot_ids = jnp.where(same_agg, 0, jnp.arange(1, 7, dtype=jnp.int32)[None, :])
    slot_ids = jnp.concatenate([jnp.zeros((elems, 1), jnp.int32), slot_ids], axis=1)
    agg_hot = (
        (agg_map - device * aggs_here)[:, None] == jnp.arange(aggs_here, dtype=jnp.int32)
    ).astype(jnp.float32)
    per_element = jnp.einsum("eji,ej->ei", prolong, residual, preferred_element_type=jnp.float32)
    restr = jnp.dot(agg_hot.T, per_element, precision=lax.Precision.HIGHEST).astype(jnp.bfloat16)
    agg_counter = jnp.arange(aggs_here, dtype=jnp.int32)
    earlier = (owners[None, :] == owners[:, None]) & (agg_counter[None, :] < agg_counter[:, None])
    within = jnp.sum(earlier.astype(jnp.int32), axis=1)
    send_slot = owners * per_owner + within
    select = (
        jnp.arange(size_z * per_owner, dtype=jnp.int32)[:, None] == send_slot[None, :]
    ).astype(jnp.bfloat16)
    heads, tails = coarse_kernel(
        jnp.stack(columns, axis=1).reshape(-1),
        slot_ids.reshape(-1),
        agg_map - device * aggs_here,
        send_slot,
        prolong,
        faces,
        jacobian,
        size_z * per_owner,
        aggs_here,
    )
    send_restr = jnp.dot(select, restr, preferred_element_type=jnp.float32).astype(jnp.bfloat16)
    heads = lax.all_to_all(heads, "gz", split_axis=0, concat_axis=0, tiled=True)
    tails = lax.all_to_all(tails, "gz", split_axis=0, concat_axis=0, tiled=True)
    restricted = lax.all_to_all(send_restr, "gz", split_axis=0, concat_axis=0, tiled=True)
    rest = width - heads.shape[3]
    tails = tails[:, :, : 7 * rest].reshape(-1, width, 7, rest).transpose(0, 2, 1, 3)
    return (jnp.concatenate([heads, tails], axis=3), restricted)


def solution(mesh):
    return jax.shard_map(
        body,
        mesh=mesh,
        in_specs=(
            P(("gx", "gy", "gz"), None, None, None),
            P(("gx", "gy", "gz"), None, None),
            P(("gx", "gy", "gz"), None),
            P(("gx", "gy", "gz"), None),
            P(("gx", "gy", "gz")),
            P(("gx", "gy", "gz")),
        ),
        out_specs=(P(("gx", "gy", "gz"), None, None, None), P(("gx", "gy", "gz"), None)),
        check_vma=False,
    )
```

time: 277 us -> 160 us (0.58)
  matrix products: 111 us -> 7.16 us
  Pallas kernels: 0 us -> 59.5 us
  local copies, waits for them, and re-layouts: 84.6 us -> 28.6 us
  waiting for transfers between devices: 52.4 us -> 22.7 us
  blocking collectives: 0 us -> 12 us
    dot_general x5 -> x0, matrix products: 104 us -> none  [the longest x2 67.3 us: body(): jnp.einsum('ea,eds,edik->asik', agg_hot, slot_hot, triple, precision=lax....]
    pallas_call x0 -> x1, Pallas kernels: none -> 59.5 us  [coarse_kernel(): pl.pallas_call(kernel, grid_spec=pltpu.PrefetchScalarGridSpec(num_scalar_...]
    transpose x1 -> x0, local copies, waits for them, and re-layouts: 38.7 us -> none  [body(): jnp.einsum('eji,edjk->edik', prolong, products, preferred_element_type=jn...]
    all_to_all x1, waiting for transfers between devices: 44.7 us -> 21.9 us  [body(): heads = lax.all_to_all(heads, 'gz', split_axis=0, concat_axis=0, tiled=True)]
    all_to_all x0 -> x1, blocking collectives: none -> 12 us  [body(): tails = lax.all_to_all(tails, 'gz', split_axis=0, concat_axis=0, tiled=True)]
    unnamed x22 -> x20, local copies, waits for them, and re-layouts: 15.2 us -> 5.59 us
    ppermute x6, waiting for transfers between devices: 7.67 us -> 0.83 us  [from_behind(): lax.ppermute(value, axis, [(source, source + steps) for source in range(i...]
    reshape x1 -> x9, local copies, waits for them, and re-layouts: 21.7 us -> 17.5 us  [the longest x6 15.6 us: body(): faces.append(fetched.reshape(face_count, width, width))]
  transfers between devices with their start and end apart: 8 -> 8, of which waited for: 2 -> 2; matrix products, arithmetic and copies ran while one was open for 68% -> 17% of each run, Pallas kernels for 0% -> 37%
where the time goes in v1:
time: 160 us; the launch traced here: 159 us
  Pallas kernels  59.5 us (37%)
  local copies, waits for them, and re-layouts  28.6 us (18%)
  starting transfers between devices  25.4 us (16%)
  waiting for transfers between devices  22.7 us (14%)
  blocking collectives  12 us (8%)
  matrix products  7.16 us (4%)
  other arithmetic  3.01 us (2%)
    pallas_call x1, Pallas kernels, coarse_kernel(): pl.pallas_call(kernel, grid_spec=pltpu.PrefetchScalarGridSpec(num_scalar_...  59.5 us
    all_to_all x1, waiting for transfers between devices, body(): heads = lax.all_to_all(heads, 'gz', split_axis=0, concat_axis=0, tiled=True)  21.9 us
    ppermute x6, starting transfers between devices, from_behind(): lax.ppermute(value, axis, [(source, source + steps) for source in range(i...  16.1 us
    reshape x6, local copies, waits for them, and re-layouts, body(): faces.append(fetched.reshape(face_count, width, width))  15.6 us
    all_to_all x1, blocking collectives, body(): tails = lax.all_to_all(tails, 'gz', split_axis=0, concat_axis=0, tiled=True)  12 us
    all_to_all x1, starting transfers between devices, body(): lax.all_to_all(send_restr, 'gz', split_axis=0, concat_axis=0, tiled=True)  5.77 us
    unnamed x20, local copies, waits for them, and re-layouts  5.59 us
    dot_general x6, matrix products, body(): jnp.dot(pack_select, flat_blocks, preferred_element_type=jnp.float32)  5.5 us
  transfers between devices with their start and end apart: 8, of which 2 were waited for; matrix products, arithmetic and copies ran while one was open for 17% of the time, Pallas kernels for 37%

profile of v1, /device:TPU:0, one launch (start us, length us, event | category | flops | bytes accessed | tf_op | source)
XLA Modules:
  0.0 159.3 jit_solution(4625579498449140381)
XLA Ops:
  0.7 0.7 compare_select_fusion
  1.4 0.1 copy.65
  1.5 0.1 reshape.327
  1.6 1.6 gather_fusion
  3.2 0.1 reshape.326
  3.3 0.1 copy.66
  3.3 0.1 and_select_fusion
  3.4 0.1 copy.73
  3.5 0.1 reduce-window.52
  3.6 0.1 add_reduce_fusion.1
  3.7 2.9 %copy.75.p_ref = bf16[32,135,135]{2,1,0:T(8,128)(2,1)S(1)} copy(bf16[32,135,135]{2,0,1:T(8,128)(2,1)} %param.7) | data formatting | bytes 2332800 | tf_op args[1]
  6.6 2.1 %reshape.317 = bf16[32,18225]{1,0:T(8,128)(2,1)S(1)} reshape(bf16[32,135,135]{2,1,0:T(8,128)(2,1)S(1)} %copy.75.p_ref) | data formatting | bytes 2332800 | tf_op jit(solution)/shard_map/reshape | solution.py:135
  8.7 1.1 convolution_convert_fusion.1
  9.8 5.8 %collective-permute-start.4 = (bf16[16,18225]{1,0:T(8,128)(2,1)}, bf16[16,18225]{1,0:T(8,128)(2,1)}, u32[]{:S(2)}, u32[]{:S(2)}) collective-permute-start(bf16[16,18225]{1,0:T(8,128)(2,1)} %convolution_convert_fusion.1), channel_id=1, source_target_pairs={{0,1},{1,2},{2,3},{4,5},{5,6},{6,7},{8,9},{9,10},{10,11},{12,13},{... | collective-permute-start | bytes 1749608 | tf_op jit(solution)/shard_map/ppermute | solution.py:16
  15.6 0.1 copy.74
  15.7 0.1 add_reduce_fusion
  15.8 1.1 convolution_convert_fusion
  16.9 1.3 collective-permute-start.5
  18.2 0.1 copy.68
  18.4 0.1 add_reduce_fusion.5
  18.5 1.0 convolution_convert_fusion.5
  19.5 2.2 %collective-permute-start = (bf16[8,18225]{1,0:T(8,128)(2,1)}, bf16[8,18225]{1,0:T(8,128)(2,1)}, u32[]{:S(2)}, u32[]{:S(2)}) collective-permute-start(bf16[8,18225]{1,0:T(8,128)(2,1)} %convolution_convert_fusion.5), channel_id=1, source_target_pairs={{0,16},{1,17},{2,18},{3,19},{4,20},{5,21},{6,22},{7,23},{8,24},{9,... | collective-permute-start | bytes 874808 | tf_op jit(solution)/shard_map/ppermute | solution.py:16
  21.7 0.1 copy.70
  21.8 0.1 add_reduce_fusion.4
  21.9 1.0 convolution_convert_fusion.4
  22.9 1.3 collective-permute-start.1
  24.2 0.1 copy.71
  24.4 0.1 add_reduce_fusion.3
  24.5 1.0 convolution_convert_fusion.3
  25.5 4.1 %collective-permute-start.2 = (bf16[8,18225]{1,0:T(8,128)(2,1)}, bf16[8,18225]{1,0:T(8,128)(2,1)}, u32[]{:S(2)}, u32[]{:S(2)}) collective-permute-start(bf16[8,18225]{1,0:T(8,128)(2,1)} %convolution_convert_fusion.3), channel_id=1, source_target_pairs={{0,4},{4,8},{8,12},{1,5},{5,9},{9,13},{2,6},{6,10},{10,14},{3,7},{... | collective-permute-start | bytes 874808 | tf_op jit(solution)/shard_map/ppermute | solution.py:16
  29.6 0.2 convert_reduce_fusion.6
  29.8 1.3 fusion.3
  31.1 0.3 convolution_convert_fusion.7
  31.4 0.1 fusion
  31.5 0.6 copy.78
  32.1 5.8 %all-to-all-start.2 = ((bf16[4,1,135]{2,1,0:T(2,128)(2,1)}), bf16[4,1,135]{2,1,0:T(2,128)(2,1)S(1)}, u32[]{:S(2)}, u32[]{:S(2)}) async-start(bf16[4,1,135]{2,1,0:T(2,128)(2,1)} %copy.78), calls=%async_computation.2 | async-start | bytes 8192 | tf_op jit(solution)/shard_map/all_to_all | solution.py:192
  37.9 0.1 copy.72
  38.0 0.1 add_reduce_fusion.2
  38.2 0.3 convolution_convert_fusion.2
  38.5 0.2 convert_reduce_fusion.2
  38.6 0.2 convert_reduce_fusion
  38.9 1.5 collective-permute-start.3
  40.3 0.2 convert_reduce_fusion.4
  40.6 0.1 copy.64
  40.7 0.7 reshape.315.col_ref
  41.3 0.1 copy.84
  41.4 0.1 concatenate.6.clone
  41.5 0.7 reshape.316.slot_ref
  42.2 2.4 %reshape.318.refs_0_ = bf16[8,135,135]{2,1,0:T(8,128)(2,1)} reshape(bf16[8,18225]{1,0:T(8,128)(2,1)} %collective-permute-done) | data formatting | bytes 583200 | tf_op jit(solution)/shard_map/reshape | solution.py:159
  44.6 2.4 %reshape.319.refs_1_ = bf16[8,135,135]{2,1,0:T(8,128)(2,1)} reshape(bf16[8,18225]{1,0:T(8,128)(2,1)} %collective-permute-done.1) | data formatting | bytes 583200 | tf_op jit(solution)/shard_map/reshape | solution.py:159
  47.0 2.4 %reshape.320.refs_2_ = bf16[8,135,135]{2,1,0:T(8,128)(2,1)} reshape(bf16[8,18225]{1,0:T(8,128)(2,1)} %collective-permute-done.2) | data formatting | bytes 583200 | tf_op jit(solution)/shard_map/reshape | solution.py:159
  49.5 0.8 collective-permute-done.3
  50.3 1.5 reshape.321.refs_3_
  51.8 3.4 %reshape.322.refs_4_ = bf16[16,135,135]{2,1,0:T(8,128)(2,1)} reshape(bf16[16,18225]{1,0:T(8,128)(2,1)} %collective-permute-done.4) | data formatting | bytes 1166400 | tf_op jit(solution)/shard_map/reshape | solution.py:159
  55.2 3.4 %reshape.323.refs_5_ = bf16[16,135,135]{2,1,0:T(8,128)(2,1)} reshape(bf16[16,18225]{1,0:T(8,128)(2,1)} %collective-permute-done.5) | data formatting | bytes 1166400 | tf_op jit(solution)/shard_map/reshape | solution.py:159
  58.6 59.5 %shard_map.77 = (bf16[4,7,135,128]{3,2,1,0:T(8,128)(2,1)}, bf16[4,135,128]{2,1,0:T(8,128)(2,1)}) custom-call(s32[224]{0:T(256)} %reshape.315.col_ref, s32[224]{0:T(256)} %reshape.316.slot_ref, s32[32]{0:T(128)} %copy-done.5, s32[4]{0:T(128)} %copy-done.6, bf16[32,135,135]{2,1,0:T(8,128)(2,1)} %copy-done.2, bf16[8,135,135]{2,1,0:T(8,128)(2,1)} %reshape.318.refs_0_, ...), custom_call_target="tpu_custom_call" | custom-call | tf_op jit(solution)/shard_map/pallas_call | solution.py:95
  118.0 12.0 %all_to_all.22 = bf16[4,135,128]{2,1,0:T(8,128)(2,1)S(1)} all-to-all(bf16[4,135,128]{2,1,0:T(8,128)(2,1)} %get-tuple-element.5), channel_id=1, replica_groups=mesh['gx'=2,'gy'=4,'gz'=4] {'gz'}, dimensions={0} | all-to-all | bytes 276480 | tf_op jit(solution)/shard_map/all_to_all | solution.py:191
  130.1 3.5 %all-to-all-start = ((bf16[4,7,135,128]{3,2,1,0:T(8,128)(2,1)}), bf16[4,7,135,128]{3,2,1,0:T(8,128)(2,1)S(1)}, u32[]{:S(2)}, u32[]{:S(2)}) async-start(bf16[4,7,135,128]{3,2,1,0:T(8,128)(2,1)} %get-tuple-element.4), calls=%async_computation | async-start | bytes 1949696 | tf_op jit(solution)/shard_map/all_to_all | solution.py:190
  133.6 0.6 copy.94
  134.2 0.2 copy.76
  134.3 0.6 copy.77
  134.9 21.9 %all-to-all-done = bf16[4,7,135,128]{3,2,1,0:T(8,128)(2,1)S(1)} async-done(((bf16[4,7,135,128]{3,2,1,0:T(8,128)(2,1)}), bf16[4,7,135,128]{3,2,1,0:T(8,128)(2,1)S(1)}, u32[]{:S(2)}, u32[]{:S(2)}) %all-to-all-start) | async-done | bytes 967712 | tf_op jit(solution)/shard_map/all_to_all | solution.py:190
  156.8 0.4 pad_maximum_fusion
  157.3 2.0 %copy.79 = bf16[4,7,135,135]{3,0,2,1:T(4,128)(2,1)} copy(bf16[4,7,135,135]{3,2,1,0:T(8,128)(2,1)S(1)} %pad_maximum_fusion) | data formatting | bytes 2041200
  (39 shorter events, 0.5 us)
Async XLA Ops:
  0.6 29.2 %copy-start = (bf16[32,135]{1,0:T(8,128)(2,1)S(1)}, bf16[32,135]{1,0:T(8,128)(2,1)}, u32[]{:S(2)}) copy-start(bf16[32,135]{1,0:T(8,128)(2,1)} %param.8) | copy-start | bytes 25924
  0.6 0.9 copy-start.1
  6.6 2.1 %copy-start.2 = (bf16[32,135,135]{2,1,0:T(8,128)(2,1)}, bf16[32,135,135]{2,1,0:T(8,128)(2,1)S(1)}, u32[]{:S(2)}) copy-start(bf16[32,135,135]{2,1,0:T(8,128)(2,1)S(1)} %copy.75.p_ref) | copy-start | bytes 3499204
  9.8 42.0 %collective-permute-start.4 = (bf16[16,18225]{1,0:T(8,128)(2,1)}, bf16[16,18225]{1,0:T(8,128)(2,1)}, u32[]{:S(2)}, u32[]{:S(2)}) collective-permute-start(bf16[16,18225]{1,0:T(8,128)(2,1)} %convolution_convert_fusion.1), channel_id=1, source_target_pairs={{0,1},{1,2},{2,3},{4,5},{5,6},{6,7},{8,9},{9,10},{10,11},{12,13},{... | collective-permute-start | bytes 1749608 | tf_op jit(solution)/shard_map/ppermute | solution.py:16
  16.9 38.2 %collective-permute-start.5 = (bf16[16,18225]{1,0:T(8,128)(2,1)}, bf16[16,18225]{1,0:T(8,128)(2,1)}, u32[]{:S(2)}, u32[]{:S(2)}) collective-permute-start(bf16[16,18225]{1,0:T(8,128)(2,1)} %convolution_convert_fusion), channel_id=1, source_target_pairs={{1,0},{2,1},{3,2},{5,4},{6,5},{7,6},{9,8},{10,9},{11,10},{13,12},{... | collective-permute-start | bytes 1749608 | tf_op jit(solution)/shard_map/ppermute | solution.py:16
  19.5 19.3 %collective-permute-start = (bf16[8,18225]{1,0:T(8,128)(2,1)}, bf16[8,18225]{1,0:T(8,128)(2,1)}, u32[]{:S(2)}, u32[]{:S(2)}) collective-permute-start(bf16[8,18225]{1,0:T(8,128)(2,1)} %convolution_convert_fusion.5), channel_id=1, source_target_pairs={{0,16},{1,17},{2,18},{3,19},{4,20},{5,21},{6,22},{7,23},{8,24},{9,... | collective-permute-start | bytes 874808 | tf_op jit(solution)/shard_map/ppermute | solution.py:16
  21.9 7.7 %copy-start.7 = (s32[4]{0:T(128)S(1)}, s32[4]{0:T(128)}, u32[]{:S(2)}) copy-start(s32[4]{0:T(128)} %param.11) | copy-start | bytes 52
  21.9 7.9 %copy-start.3 = (bf16[32,135,135]{2,0,1:T(8,128)(2,1)S(1)}, bf16[32,135,135]{2,0,1:T(8,128)(2,1)}, u32[]{:S(2)}) copy-start(bf16[32,135,135]{2,0,1:T(8,128)(2,1)} %param.7) | copy-start | bytes 3499204
  22.9 21.7 %collective-permute-start.1 = (bf16[8,18225]{1,0:T(8,128)(2,1)}, bf16[8,18225]{1,0:T(8,128)(2,1)}, u32[]{:S(2)}, u32[]{:S(2)}) collective-permute-start(bf16[8,18225]{1,0:T(8,128)(2,1)} %convolution_convert_fusion.4), channel_id=1, source_target_pairs={{16,0},{17,1},{18,2},{19,3},{20,4},{21,5},{22,6},{23,7},{24,8},{25... | collective-permute-start | bytes 874808 | tf_op jit(solution)/shard_map/ppermute | solution.py:16
  25.5 21.6 %collective-permute-start.2 = (bf16[8,18225]{1,0:T(8,128)(2,1)}, bf16[8,18225]{1,0:T(8,128)(2,1)}, u32[]{:S(2)}, u32[]{:S(2)}) collective-permute-start(bf16[8,18225]{1,0:T(8,128)(2,1)} %convolution_convert_fusion.3), channel_id=1, source_target_pairs={{0,4},{4,8},{8,12},{1,5},{5,9},{9,13},{2,6},{6,10},{10,14},{3,7},{... | collective-permute-start | bytes 874808 | tf_op jit(solution)/shard_map/ppermute | solution.py:16
  29.6 1.5 copy-start.5
  29.8 1.6 copy-start.6
  29.8 8.1 %copy-start.4 = (s32[32,6]{0,1:T(8,128)S(1)}, s32[32,6]{0,1:T(8,128)}, u32[]{:S(2)}) copy-start(s32[32,6]{0,1:T(8,128)} %param.9) | copy-start | bytes 2308
  32.1 85.9 %all-to-all-start.2 = ((bf16[4,1,135]{2,1,0:T(2,128)(2,1)}), bf16[4,1,135]{2,1,0:T(2,128)(2,1)S(1)}, u32[]{:S(2)}, u32[]{:S(2)}) async-start(bf16[4,1,135]{2,1,0:T(2,128)(2,1)} %copy.78), calls=%async_computation.2 | async-start | bytes 8192 | tf_op jit(solution)/shard_map/all_to_all | solution.py:192
  38.9 11.4 %collective-permute-start.3 = (bf16[8,18225]{1,0:T(8,128)(2,1)S(1)}, bf16[8,18225]{1,0:T(8,128)(2,1)S(1)}, u32[]{:S(2)}, u32[]{:S(2)}) collective-permute-start(bf16[8,18225]{1,0:T(8,128)(2,1)S(1)} %convolution_convert_fusion.2), channel_id=1, source_target_pairs={{4,0},{8,4},{12,8},{5,1},{9,5},{13,9},{6,2},{10,6},{14,10},{7,3},{... | collective-permute-start | bytes 874808 | tf_op jit(solution)/shard_map/ppermute | solution.py:16
  130.1 26.8 %all-to-all-start = ((bf16[4,7,135,128]{3,2,1,0:T(8,128)(2,1)}), bf16[4,7,135,128]{3,2,1,0:T(8,128)(2,1)S(1)}, u32[]{:S(2)}, u32[]{:S(2)}) async-start(bf16[4,7,135,128]{3,2,1,0:T(8,128)(2,1)} %get-tuple-element.4), calls=%async_computation | async-start | bytes 1949696 | tf_op jit(solution)/shard_map/all_to_all | solution.py:190

commit v2 on v0

v2 whole, which is shorter than its diff:
```python
import jax
import jax.numpy as jnp
from jax import lax
from jax.experimental import pallas as pl
from jax.experimental.pallas import tpu as pltpu
from jax.sharding import PartitionSpec as P


LX = 4
LY = 4
LZ = 2
LANES = 128
UNROLL = 4


def from_behind(value, axis, steps):
    count = lax.axis_size(axis)
    initial, last = (max(0, -steps), min(count, count - steps))
    return lax.ppermute(value, axis, [(source, source + steps) for source in range(initial, last)])


def whole():
    return pl.BlockSpec(memory_space=pltpu.VMEM)


def params():
    return pltpu.CompilerParams(vmem_limit_bytes=56 << 20)


def cost(pairs, width):
    return pl.CostEstimate(
        flops=pairs * 96 * width * width * width,
        bytes_accessed=pairs * 4 * width * width,
        transcendentals=0,
    )


def pack_kernel(picks, prolong, counts):
    _, width, _ = prolong.shape
    rest = width - LANES

    def kernel(pick_ref, p_ref, *outs):
        for d, (out, count) in enumerate(zip(outs, counts)):
            for n in range(count):
                block = p_ref[pick_ref[d, n]]
                out[n] = block[:, :LANES]
                out[count, :, n * rest : (n + 1) * rest] = block[:, LANES:]

    return pl.pallas_call(
        kernel,
        grid_spec=pltpu.PrefetchScalarGridSpec(
            num_scalar_prefetch=1,
            grid=(1,),
            in_specs=[whole()],
            out_specs=[whole()] * len(counts),
        ),
        out_shape=[jax.ShapeDtypeStruct((n + 1, width, LANES), prolong.dtype) for n in counts],
        compiler_params=params(),
    )(picks, prolong)


def spread(j_ref, near, far):
    _, width, elems, _ = j_ref.shape
    step_rows = 5 if width % 5 == 0 else 1
    rest = width - LANES

    @pl.loop(0, width // step_rows)
    def _(c):
        part = j_ref[0, pl.ds(c * step_rows, step_rows)].astype(jnp.float32)
        part = part.reshape(step_rows * elems, width)
        rows = pl.ds(pl.multiple_of(c * step_rows * elems, 8), step_rows * elems)
        near[rows, :] = part[:, :LANES]
        far[rows, :rest] = part[:, LANES:]


def own_block(near, far, e, width, elems):
    rows = pl.ds(e, width, stride=elems)
    both = jnp.concatenate([near[rows, :], far[rows, :]], axis=1)
    return both[:, :width].astype(jnp.bfloat16)


def mul(a, b):
    return jnp.dot(a, b, preferred_element_type=jnp.float32)


def spread_scratch(width, elems):
    return [pltpu.VMEM((width * elems, LANES), jnp.float32)] * 2


def jac_spec(width, elems, first):
    return pl.BlockSpec((1, width, elems, width), lambda k, *_: (first + k, 0, 0, 0))


def own_kernel(table, prolong, jac, aggs_here):
    elems, width, _ = prolong.shape

    def kernel(table_ref, p_ref, j_ref, total, flipped, near, far):
        total[...] = jnp.zeros_like(total)
        spread(j_ref, near, far)

        @pl.loop(0, elems // UNROLL)
        def _(group):
            at = [group * UNROLL + u for u in range(UNROLL)]
            products = [
                mul(own_block(near, far, e, width, elems), p_ref[e]).astype(jnp.bfloat16)
                for e in at
            ]
            turned = [p_ref[e].astype(jnp.float32).T.astype(flipped.dtype) for e in at]
            triples = [mul(t, product) for t, product in zip(turned, products)]
            for e, t, triple in zip(at, turned, triples):
                flipped[e] = t
                total[table_ref[7, e]] += triple

    return pl.pallas_call(
        kernel,
        grid_spec=pltpu.PrefetchScalarGridSpec(
            num_scalar_prefetch=1,
            grid=(1,),
            in_specs=[whole(), jac_spec(width, elems, 0)],
            out_specs=[whole(), whole()],
            scratch_shapes=spread_scratch(width, elems),
        ),
        out_shape=[
            jax.ShapeDtypeStruct((aggs_here, width, width), jnp.float32),
            jax.ShapeDtypeStruct(prolong.shape, prolong.dtype),
        ],
        cost_estimate=cost(elems, width),
        compiler_params=params(),
    )(table, prolong, jac)


def side_kernel(table, dest, prolong, flipped, carry, faces, jac, first, out_slots, restr=None):
    elems, width, _ = prolong.shape
    aggs_here = carry.shape[0]
    rest = width - LANES
    count = len(faces)
    zero_block = elems + max(face.shape[0] for face in faces) - 1
    final = restr is not None
    emitted = range(0 if final else 1, count + 1)
    rows_out = len(emitted)

    def kernel(table_ref, dest_ref, p_ref, t_ref, carry_ref, *refs):
        face_refs, refs = refs[:count], refs[count:]
        if final:
            restr_ref, refs = refs[0], refs[1:]
        j_ref, out, refs = refs[0], refs[1], refs[2:]
        if not final:
            next_ref, refs = refs[0], refs[1:]
        pool, near, far, total = refs
        k = pl.program_id(0)

        @pl.when(k == 0)
        def _():
            out[...] = jnp.zeros_like(out)
            total[...] = jnp.zeros_like(total)
            pool[zero_block] = jnp.zeros((width, width), pool.dtype)

            @pl.loop(0, aggs_here)
            def _(a):
                total[a, 0] = carry_ref[a]

            @pl.loop(0, elems)
            def _(e):
                pool[e] = p_ref[e]

        for d, face_ref in enumerate(face_refs):

            @pl.when(k == d)
            def _(face_ref=face_ref):
                last = face_ref.shape[0] - 1
                for n in range(last):
                    pool[elems + n, :, :LANES] = face_ref[n]
                    pool[elems + n, :, LANES:] = face_ref[last, :, n * rest : (n + 1) * rest]

        spread(j_ref, near, far)

        @pl.loop(0, elems // UNROLL)
        def _(group):
            at = [group * UNROLL + u for u in range(UNROLL)]
            codes = [table_ref[first + k, e] for e in at]
            products = [
                mul(own_block(near, far, e, width, elems), pool[code // 2]).astype(jnp.bfloat16)
                for e, code in zip(at, codes)
            ]
            triples = [mul(t_ref[e], product) for e, product in zip(at, products)]
            for e, code, triple in zip(at, codes, triples):
                total[table_ref[7, e], jnp.where(code % 2 == 1, 0, k + 1)] += triple

        @pl.when(k == count - 1)
        def _():
            for a in range(aggs_here):
                to = dest_ref[a]
                for i, s in enumerate(emitted):
                    row = total[a, s].astype(jnp.bfloat16)
                    out[to, i] = row[:, :LANES]
                    out[to, rows_out, :, i * rest : (i + 1) * rest] = row[:, LANES:]
                if final:
                    lane = rows_out * rest
                    out[to, rows_out, :, lane : lane + 1] = restr_ref[:, a : a + 1]
                else:
                    next_ref[a] = total[a, 0]

    out_shape = [jax.ShapeDtypeStruct((out_slots, rows_out + 1, width, LANES), jnp.bfloat16)]
    if not final:
        out_shape.append(jax.ShapeDtypeStruct(carry.shape, carry.dtype))
    inputs = [prolong, flipped, carry, *faces] + ([restr] if final else [])
    return pl.pallas_call(
        kernel,
        grid_spec=pltpu.PrefetchScalarGridSpec(
            num_scalar_prefetch=2,
            grid=(count,),
            in_specs=[whole()] * len(inputs) + [jac_spec(width, elems, first)],
            out_specs=[whole()] * len(out_shape),
            scratch_shapes=[pltpu.VMEM((zero_block + 1, width, width), jnp.bfloat16)]
            + spread_scratch(width, elems)
            + [pltpu.VMEM((aggs_here, count + 1, width, width), jnp.float32)],
        ),
        out_shape=out_shape,
        cost_estimate=cost(elems * count, width),
        compiler_params=params(),
    )(table, dest, *inputs, jac)


def body(jacobian, prolong, residual, neighbours, agg_map, owners):
    elems = jacobian.shape[0]
    width = prolong.shape[1]
    aggs_here = owners.shape[0]
    rest = width - LANES
    size_x = lax.axis_size("gx")
    size_y = lax.axis_size("gy")
    size_z = lax.axis_size("gz")
    per_owner = aggs_here // 4
    out_slots = size_z * per_owner
    device = (lax.axis_index("gx") * size_y + lax.axis_index("gy")) * size_z + lax.axis_index("gz")
    nbr = neighbours.T
    local_ids = nbr - device * elems
    on_device = (local_ids >= 0) & (local_ids < elems)
    is_valid = nbr >= 0
    face_sizes = (LY * LZ, LX * LZ, LX * LY)
    ids = jnp.arange(elems, dtype=jnp.int32)
    agg_local = agg_map - device * aggs_here

    off_side = jnp.logical_not(on_device)
    before = ids[None, :] < ids[:, None]
    face_rank = jnp.sum((off_side[:, None, :] & before[None]).astype(jnp.int32), axis=2)
    ranks = jnp.arange(max(face_sizes), dtype=jnp.int32)
    chosen = off_side[:, None, :] & (face_rank[:, None, :] == ranks[None, :, None])
    by_side = jnp.sum(jnp.where(chosen, ids, 0), axis=2)

    off_valid = off_side & is_valid
    lower = off_valid[:, None, :] & (nbr[:, None, :] < nbr[:, :, None])
    position = jnp.sum(lower.astype(jnp.int32), axis=2)
    zero_xy = elems + max(face_sizes[:2])
    zero_z = elems + face_sizes[2]
    zeros = jnp.where(jnp.arange(6) < 4, zero_xy, zero_z)[:, None].astype(jnp.int32)
    column = jnp.where(on_device, local_ids, elems + position)
    column = jnp.where(is_valid, column, zeros)
    near_agg = jnp.sum(jnp.where(local_ids[:, :, None] == ids, agg_local, 0), axis=2)
    same_agg = on_device & (near_agg == agg_local[None, :])
    codes = column * 2 + same_agg.astype(jnp.int32)
    table = jnp.concatenate([ids[None] * 2 + 1, codes, agg_local[None]], axis=0)

    sends = [d ^ 1 for d in range(6)]
    if size_x == 2:
        swap = jnp.where(lax.axis_index("gx") == 0, by_side[1], by_side[0])
        picks = jnp.stack([by_side[5], by_side[4], by_side[3], by_side[2], swap])
        counts = [face_sizes[2]] * 2 + [face_sizes[1]] * 2 + [face_sizes[0]]
    else:
        picks = jnp.stack([by_side[sends[d]] for d in (4, 5, 2, 3, 0, 1)])
        counts = [face_sizes[d // 2] for d in (4, 5, 2, 3, 0, 1)]
    packed = pack_kernel(picks, prolong, counts)
    z_up = from_behind(packed[0], "gz", 1)
    z_down = from_behind(packed[1], "gz", -1)
    z_faces = [z_up, z_down]
    y_faces = [from_behind(packed[2], "gy", 1), from_behind(packed[3], "gy", -1)]
    if size_x == 2:
        x_faces = [lax.ppermute(packed[4], "gx", [(0, 1), (1, 0)])] * 2
    else:
        x_faces = [from_behind(packed[4], "gx", 1), from_behind(packed[5], "gx", -1)]

    agg_hot = (agg_local[:, None] == jnp.arange(aggs_here, dtype=jnp.int32)).astype(jnp.float32)
    per_element = jnp.einsum("eji,ej->ei", prolong, residual, preferred_element_type=jnp.float32)
    restr = jnp.dot(per_element.T, agg_hot, precision=lax.Precision.HIGHEST).astype(jnp.bfloat16)

    agg_counter = jnp.arange(aggs_here, dtype=jnp.int32)
    earlier = (owners[None, :] == owners[:, None]) & (agg_counter[None, :] < agg_counter[:, None])
    within = jnp.sum(earlier.astype(jnp.int32), axis=1)
    dest = owners * per_owner + within

    jac = jnp.transpose(jacobian, (1, 2, 0, 3))
    carry, flipped = own_kernel(table, prolong, jac, aggs_here)
    first, carry = side_kernel(
        table, dest, prolong, flipped, carry, x_faces + y_faces, jac, 1, out_slots
    )
    first = lax.all_to_all(first, "gz", split_axis=0, concat_axis=0, tiled=True)
    (second,) = side_kernel(
        table, dest, prolong, flipped, carry, z_faces, jac, 5, out_slots, restr=restr
    )
    second = lax.all_to_all(second, "gz", split_axis=0, concat_axis=0, tiled=True)

    def tails(part, rows):
        packed_tail = part[:, rows, :, : rows * rest]
        return packed_tail.reshape(-1, width, rows, rest).transpose(0, 2, 1, 3)

    first_tails, second_tails = tails(first, 4), tails(second, 3)
    heads = jnp.concatenate([second[:, :1], first[:, :4], second[:, 1:3]], axis=1)
    ends = jnp.concatenate([second_tails[:, :1], first_tails, second_tails[:, 1:]], axis=1)
    restricted = second[:, 3, :, 3 * rest]
    return (jnp.concatenate([heads, ends], axis=3), restricted)


def solution(mesh):
    return jax.shard_map(
        body,
        mesh=mesh,
        in_specs=(
            P(("gx", "gy", "gz"), None, None, None),
            P(("gx", "gy", "gz"), None, None),
            P(("gx", "gy", "gz"), None),
            P(("gx", "gy", "gz"), None),
            P(("gx", "gy", "gz")),
            P(("gx", "gy", "gz")),
        ),
        out_specs=(P(("gx", "gy", "gz"), None, None, None), P(("gx", "gy", "gz"), None)),
        check_vma=False,
    )
```

time: 277 us -> 120 us (0.43)
  matrix products: 111 us -> 1.53 us
  local copies, waits for them, and re-layouts: 84.6 us -> 15.4 us
  Pallas kernels: 0 us -> 60.6 us
  waiting for transfers between devices: 52.4 us -> 14.1 us
    dot_general x13 -> x1, matrix products: 109 us -> 0.25 us  [body(): jnp.dot(per_element.T, agg_hot, precision=lax.Precision.HIGHEST)]
    pallas_call x0 -> x4, Pallas kernels: none -> 60.6 us  [the longest x2 45.9 us: side_kernel(): pl.pallas_call(kernel, grid_spec=pltpu.PrefetchScalarGridSpec(num_scalar_...]
    transpose x1 -> x0, local copies, waits for them, and re-layouts: 38.7 us -> none  [body(): jnp.einsum('eji,edjk->edik', prolong, products, preferred_element_type=jn...]
    all_to_all x2, waiting for transfers between devices: 44.7 us -> 14 us  [the longest x1 14 us: body(): lax.all_to_all(second, 'gz', split_axis=0, concat_axis=0, tiled=True)]
    reshape x2 -> x0, local copies, waits for them, and re-layouts: 25 us -> none  [the longest x1 21.7 us: body(): gathered = gathered.reshape(elems, 7, width, width)]
    unnamed x22 -> x18, local copies, waits for them, and re-layouts: 15.2 us -> 7.34 us
    ppermute x6 -> x4, waiting for transfers between devices: 7.67 us -> 0.01 us  [from_behind(): lax.ppermute(value, axis, [(source, source + steps) for source in range(i...]
    ppermute x6 -> x4, starting transfers between devices: 16.3 us -> 11.3 us  [from_behind(): lax.ppermute(value, axis, [(source, source + steps) for source in range(i...]
  transfers between devices with their start and end apart: 8 -> 7, of which waited for: 2 -> 1; matrix products, arithmetic and copies ran while one was open for 68% -> 5% of each run, Pallas kernels for 0% -> 47%
where the time goes in v2:
time: 120 us; the launch traced here: 119 us
  Pallas kernels  60.6 us (50%)
  starting transfers between devices  22.9 us (19%)
  local copies, waits for them, and re-layouts  15.4 us (13%)
  waiting for transfers between devices  14.1 us (12%)
  other arithmetic  4.02 us (3%)
  matrix products  1.53 us (1%)
    pallas_call x2, Pallas kernels, side_kernel(): pl.pallas_call(kernel, grid_spec=pltpu.PrefetchScalarGridSpec(num_scalar_...  45.9 us
    all_to_all x1, waiting for transfers between devices, body(): lax.all_to_all(second, 'gz', split_axis=0, concat_axis=0, tiled=True)  14 us
    ppermute x4, starting transfers between devices, from_behind(): lax.ppermute(value, axis, [(source, source + steps) for source in range(i...  11.3 us
    pallas_call x1, Pallas kernels, own_kernel(): pl.pallas_call(kernel, grid_spec=pltpu.PrefetchScalarGridSpec(num_scalar_...  10 us
    unnamed x18, local copies, waits for them, and re-layouts  7.34 us
    all_to_all x1, starting transfers between devices, body(): first = lax.all_to_all(first, 'gz', split_axis=0, concat_axis=0, tiled=True)  5.94 us
    all_to_all x1, starting transfers between devices, body(): lax.all_to_all(second, 'gz', split_axis=0, concat_axis=0, tiled=True)  5.09 us
    pallas_call x1, Pallas kernels, pack_kernel(): pl.pallas_call(kernel, grid_spec=pltpu.PrefetchScalarGridSpec(num_scalar_...  4.69 us
  transfers between devices with their start and end apart: 7, of which 1 were waited for; matrix products, arithmetic and copies ran while one was open for 5% of the time, Pallas kernels for 47%

profile of v2, /device:TPU:0, one launch (start us, length us, event | category | flops | bytes accessed | tf_op | source)
XLA Modules:
  0.0 119.3 jit_solution(2953040714216216488)
XLA Ops:
  0.6 0.0 copy-start
  0.7 0.7 fusion.9
  1.4 0.7 broadcast_subtract_fusion.1
  2.0 0.3 convert_reduce_fusion
  2.4 0.2 select_reduce_fusion.1
  2.5 4.2 %copy.53.p_ref = bf16[32,135,135]{2,1,0:T(8,128)(2,1)} copy(bf16[32,135,135]{2,0,1:T(8,128)(2,1)} %param.7) | data formatting | bytes 2332800 | tf_op args[1]
  6.8 0.0 copy-start.5
  6.8 0.0 copy-start.1
  6.8 0.6 stack.4.pick_ref
  7.4 4.7 %shard_map.78 = (bf16[17,135,128]{2,1,0:T(8,128)(2,1)}, bf16[17,135,128]{2,1,0:T(8,128)(2,1)}, bf16[9,135,128]{2,1,0:T(8,128)(2,1)}, bf16[9,135,128]{2,1,0:T(8,128)(2,1)}, bf16[9,135,128]{2,1,0:T(8,128)(2,1)}) custom-call(s32[5,16]{1,0:T(8,128)} %stack.4.pick_ref, bf16[32,135,135]{2,1,0:T(8,128)(2,1)} %copy.53.p_ref), custom_call_target="tpu_custom_call" | custom-call | tf_op jit(solution)/shard_map/pallas_call | solution.py:49
  12.1 0.0 copy-start.2
  12.1 0.5 collective-permute-start
  12.6 5.3 %collective-permute-start.1 = (bf16[9,135,128]{2,1,0:T(8,128)(2,1)}, bf16[9,135,128]{2,1,0:T(8,128)(2,1)}, u32[]{:S(2)}, u32[]{:S(2)}) collective-permute-start(bf16[9,135,128]{2,1,0:T(8,128)(2,1)} %get-tuple-element.14), channel_id=1, source_target_pairs={{0,4},{4,8},{8,12},{1,5},{5,9},{9,13},{2,6},{6,10},{10,14},{3,7},{... | collective-permute-start | bytes 933128 | tf_op jit(solution)/shard_map/ppermute | solution.py:19
  17.8 1.3 %collective-permute-start.2 = (bf16[9,135,128]{2,1,0:T(8,128)(2,1)}, bf16[9,135,128]{2,1,0:T(8,128)(2,1)}, u32[]{:S(2)}, u32[]{:S(2)}) collective-permute-start(bf16[9,135,128]{2,1,0:T(8,128)(2,1)} %get-tuple-element.15), channel_id=1, source_target_pairs={{4,0},{8,4},{12,8},{5,1},{9,5},{13,9},{6,2},{10,6},{14,10},{7,3},{... | collective-permute-start | bytes 933128 | tf_op jit(solution)/shard_map/ppermute | solution.py:19
  19.1 3.5 %collective-permute-start.3 = (bf16[17,135,128]{2,1,0:T(8,128)(2,1)}, bf16[17,135,128]{2,1,0:T(8,128)(2,1)S(1)}, u32[]{:S(2)}, u32[]{:S(2)}) collective-permute-start(bf16[17,135,128]{2,1,0:T(8,128)(2,1)} %get-tuple-element.17), channel_id=1, source_target_pairs={{0,1},{1,2},{2,3},{4,5},{5,6},{6,7},{8,9},{9,10},{10,11},{12,13},{... | collective-permute-start | bytes 1762568 | tf_op jit(solution)/shard_map/ppermute | solution.py:19
  22.6 1.3 %collective-permute-start.4 = (bf16[17,135,128]{2,1,0:T(8,128)(2,1)}, bf16[17,135,128]{2,1,0:T(8,128)(2,1)S(1)}, u32[]{:S(2)}, u32[]{:S(2)}) collective-permute-start(bf16[17,135,128]{2,1,0:T(8,128)(2,1)} %get-tuple-element.18), channel_id=1, source_target_pairs={{1,0},{2,1},{3,2},{5,4},{6,5},{7,6},{9,8},{10,9},{11,10},{13,12},{... | collective-permute-start | bytes 1762568 | tf_op jit(solution)/shard_map/ppermute | solution.py:19
  24.0 0.0 copy-done.5
  24.0 0.0 copy-done
  24.0 0.0 copy-done.1
  24.0 1.3 %fusion.3 = f32[32,1,135]{2,1,0:T(1,128)S(1)} fusion(bf16[32,135,1]{1,0,2:T(8,128)(2,1)S(1)} %bitcast.18, bf16[32,135,135]{2,0,1:T(8,128)(2,1)S(1)} %copy-done.1), kind=kOutput, calls=%fused_computation.13 | convolution fusion | flops 1166400 | bytes 1192320 | tf_op jit(solution)/shard_map/eji,ej->ei/dot_general | solution.py:282
  25.3 0.0 copy-done.2
  25.3 0.3 convert_reduce_fusion.1
  25.6 0.1 convert_add_fusion
  25.6 0.6 pad_add_fusion.table_ref
  26.2 0.0 copy-start.6
  26.2 10.0 %shard_map.77 = (f32[4,135,135]{2,1,0:T(8,128)}, bf16[32,135,135]{2,1,0:T(8,128)(2,1)}) custom-call(s32[8,32]{1,0:T(8,128)} %pad_add_fusion.table_ref, bf16[32,135,135]{2,1,0:T(8,128)(2,1)} %copy.53.p_ref, bf16[7,135,32,135]{3,2,1,0:T(8,128)(2,1)} %bitcast.23), custom_call_target="tpu_custom_call" | custom-call | flops 7558272000 | bytes 2332800 | tf_op jit(solution)/shard_map/pallas_call | solution.py:114
  36.3 0.0 copy-done.6
  36.3 0.2 convert_reduce_fusion.2
  36.4 0.5 add.35.dest_ref
  37.0 0.3 convolution_convert_fusion
  37.2 0.8 copy.54.refs_2_
  38.0 0.0 collective-permute-done.refs_0_.refs_1_
  38.0 0.0 collective-permute-done.1.refs_2_
  38.0 0.0 collective-permute-done.2.refs_3_
  38.0 28.8 %shard_map.79 = (bf16[4,5,135,128]{3,2,1,0:T(8,128)(2,1)}, f32[4,135,135]{2,1,0:T(8,128)}) custom-call(s32[8,32]{1,0:T(8,128)} %pad_add_fusion.table_ref, s32[4]{0:T(128)} %add.35.dest_ref, bf16[32,135,135]{2,1,0:T(8,128)(2,1)} %copy.53.p_ref, bf16[32,135,135]{2,1,0:T(8,128)(2,1)} %get-tuple-element.11.t_ref, f32[4,135,135]{2,1,0:T(8,128)} %get-tuple-element.12.carry_ref, ...), custom_call_target="tpu_custom_call" | custom-call | flops 30233088000 | bytes 9331200 | tf_op jit(solution)/shard_map/pallas_call | solution.py:207
  66.8 5.9 %all-to-all-start.1 = ((bf16[4,5,135,128]{3,2,1,0:T(8,128)(2,1)}), bf16[4,5,135,128]{3,2,1,0:T(8,128)(2,1)S(1)}, u32[]{:S(2)}, u32[]{:S(2)}) async-start(bf16[4,5,135,128]{3,2,1,0:T(8,128)(2,1)} %get-tuple-element.19), calls=%async_computation.1 | async-start | bytes 1392640 | tf_op jit(solution)/shard_map/all_to_all | solution.py:295
  72.7 0.0 collective-permute-done.3.refs_0_
  72.7 0.0 copy-start.3
  72.7 0.0 collective-permute-done.4.refs_1_
  72.7 0.0 copy-start.4
  72.8 0.8 copy-done.3
  73.6 0.2 copy-done.4
  73.8 17.1 %shard_map.80 = bf16[4,4,135,128]{3,2,1,0:T(8,128)(2,1)} custom-call(s32[8,32]{1,0:T(8,128)} %pad_add_fusion.table_ref, s32[4]{0:T(128)} %add.35.dest_ref, bf16[32,135,135]{2,1,0:T(8,128)(2,1)} %copy.53.p_ref, bf16[32,135,135]{2,1,0:T(8,128)(2,1)} %get-tuple-element.11.t_ref, f32[4,135,135]{2,1,0:T(8,128)} %get-tuple-element.16.carry_ref, ...), custom_call_target="tpu_custom_call" | custom-call | flops 15116544000 | bytes 4665600 | tf_op jit(solution)/shard_map/pallas_call | solution.py:207
  90.8 2.1 %copy.55 = bf16[4,4,135,128]{3,1,2,0:T(4,128)(2,1)} copy(bf16[4,4,135,128]{3,2,1,0:T(8,128)(2,1)} %shard_map.80) | data formatting | bytes 1105920 | tf_op jit(solution)/shard_map/pallas_call | solution.py:207
  92.9 0.0 all-to-all-done.1
  92.9 5.1 %all-to-all-start = ((bf16[4,4,135,128]{3,1,2,0:T(4,128)(2,1)}), bf16[4,4,135,128]{3,1,2,0:T(4,128)(2,1)S(1)}, u32[]{:S(2)}, u32[]{:S(2)}) async-start(bf16[4,4,135,128]{3,1,2,0:T(4,128)(2,1)} %copy.55), calls=%async_computation | async-start | bytes 1105920 | tf_op jit(solution)/shard_map/all_to_all | solution.py:299
  98.0 0.2 copy.59
  98.2 14.0 %all-to-all-done = bf16[4,4,135,128]{3,1,2,0:T(4,128)(2,1)S(1)} async-done(((bf16[4,4,135,128]{3,1,2,0:T(4,128)(2,1)}), bf16[4,4,135,128]{3,1,2,0:T(4,128)(2,1)S(1)}, u32[]{:S(2)}, u32[]{:S(2)}) %all-to-all-start) | async-done | bytes 552992 | tf_op jit(solution)/shard_map/all_to_all | solution.py:299
  112.3 0.3 slice.59
  112.6 0.2 copy.58
  112.8 0.1 pad_maximum_fusion.1
  112.9 0.5 copy.60
  113.4 0.3 slice.58
  113.7 0.2 slice.56
  114.0 0.4 pad_maximum_fusion
  114.4 2.0 %copy.61 = bf16[4,7,135,135]{3,0,2,1:T(4,128)(2,1)} copy(bf16[4,7,135,135]{3,2,1,0:T(8,128)(2,1)S(1)} %pad_maximum_fusion) | data formatting | bytes 2041200
  116.4 2.9 %slice_reduce_fusion = bf16[4,135]{1,0:T(4,128)(2,1)} fusion(bf16[4,4,135,128]{3,1,2,0:T(4,128)(2,1)S(1)} %all-to-all-done), kind=kLoop, calls=%fused_computation.2 | loop fusion | bytes 2160 | tf_op jit(solution)/shard_map/slice | solution.py:308
  (11 shorter events, 0.2 us)
Async XLA Ops:
  0.6 23.4 %copy-start = (bf16[32,135]{1,0:T(8,128)(2,1)S(1)}, bf16[32,135]{1,0:T(8,128)(2,1)}, u32[]{:S(2)}) copy-start(bf16[32,135]{1,0:T(8,128)(2,1)} %param.8) | copy-start | bytes 25924
  6.8 17.2 %copy-start.5 = (s32[32]{0:T(128)S(1)}, s32[32]{0:T(128)}, u32[]{:S(2)}) copy-start(s32[32]{0:T(128)} %param.10) | copy-start | bytes 388
  6.8 17.2 %copy-start.1 = (bf16[32,135,135]{2,0,1:T(8,128)(2,1)S(1)}, bf16[32,135,135]{2,0,1:T(8,128)(2,1)}, u32[]{:S(2)}) copy-start(bf16[32,135,135]{2,0,1:T(8,128)(2,1)} %param.7) | copy-start | bytes 3499204
  12.1 13.2 %copy-start.2 = (s32[32,6]{0,1:T(8,128)S(1)}, s32[32,6]{0,1:T(8,128)}, u32[]{:S(2)}) copy-start(s32[32,6]{0,1:T(8,128)} %param.9) | copy-start | bytes 2308
  12.1 25.9 %collective-permute-start = (bf16[9,135,128]{2,1,0:T(8,128)(2,1)}, bf16[9,135,128]{2,1,0:T(8,128)(2,1)}, u32[]{:S(2)}, u32[]{:S(2)}) collective-permute-start(bf16[9,135,128]{2,1,0:T(8,128)(2,1)} %get-tuple-element.13), channel_id=1, source_target_pairs={{0,16},{16,0},{1,17},{17,1},{2,18},{18,2},{3,19},{19,3},{4,20},{20... | collective-permute-start | bytes 933128 | tf_op jit(solution)/shard_map/ppermute | solution.py:277
  12.6 25.4 %collective-permute-start.1 = (bf16[9,135,128]{2,1,0:T(8,128)(2,1)}, bf16[9,135,128]{2,1,0:T(8,128)(2,1)}, u32[]{:S(2)}, u32[]{:S(2)}) collective-permute-start(bf16[9,135,128]{2,1,0:T(8,128)(2,1)} %get-tuple-element.14), channel_id=1, source_target_pairs={{0,4},{4,8},{8,12},{1,5},{5,9},{9,13},{2,6},{6,10},{10,14},{3,7},{... | collective-permute-start | bytes 933128 | tf_op jit(solution)/shard_map/ppermute | solution.py:19
  17.8 20.1 %collective-permute-start.2 = (bf16[9,135,128]{2,1,0:T(8,128)(2,1)}, bf16[9,135,128]{2,1,0:T(8,128)(2,1)}, u32[]{:S(2)}, u32[]{:S(2)}) collective-permute-start(bf16[9,135,128]{2,1,0:T(8,128)(2,1)} %get-tuple-element.15), channel_id=1, source_target_pairs={{4,0},{8,4},{12,8},{5,1},{9,5},{13,9},{6,2},{10,6},{14,10},{7,3},{... | collective-permute-start | bytes 933128 | tf_op jit(solution)/shard_map/ppermute | solution.py:19
  19.1 53.6 %collective-permute-start.3 = (bf16[17,135,128]{2,1,0:T(8,128)(2,1)}, bf16[17,135,128]{2,1,0:T(8,128)(2,1)S(1)}, u32[]{:S(2)}, u32[]{:S(2)}) collective-permute-start(bf16[17,135,128]{2,1,0:T(8,128)(2,1)} %get-tuple-element.17), channel_id=1, source_target_pairs={{0,1},{1,2},{2,3},{4,5},{5,6},{6,7},{8,9},{9,10},{10,11},{12,13},{... | collective-permute-start | bytes 1762568 | tf_op jit(solution)/shard_map/ppermute | solution.py:19
  22.6 50.1 %collective-permute-start.4 = (bf16[17,135,128]{2,1,0:T(8,128)(2,1)}, bf16[17,135,128]{2,1,0:T(8,128)(2,1)S(1)}, u32[]{:S(2)}, u32[]{:S(2)}) collective-permute-start(bf16[17,135,128]{2,1,0:T(8,128)(2,1)} %get-tuple-element.18), channel_id=1, source_target_pairs={{1,0},{2,1},{3,2},{5,4},{6,5},{7,6},{9,8},{10,9},{11,10},{13,12},{... | collective-permute-start | bytes 1762568 | tf_op jit(solution)/shard_map/ppermute | solution.py:19
  26.2 10.0 %copy-start.6 = (s32[4]{0:T(128)S(1)}, s32[4]{0:T(128)}, u32[]{:S(2)}) copy-start(s32[4]{0:T(128)} %param.11) | copy-start | bytes 52
  66.8 26.1 %all-to-all-start.1 = ((bf16[4,5,135,128]{3,2,1,0:T(8,128)(2,1)}), bf16[4,5,135,128]{3,2,1,0:T(8,128)(2,1)S(1)}, u32[]{:S(2)}, u32[]{:S(2)}) async-start(bf16[4,5,135,128]{3,2,1,0:T(8,128)(2,1)} %get-tuple-element.19), calls=%async_computation.1 | async-start | bytes 1392640 | tf_op jit(solution)/shard_map/all_to_all | solution.py:295
  72.7 0.8 copy-start.3
  72.7 1.0 copy-start.4
  92.9 19.3 %all-to-all-start = ((bf16[4,4,135,128]{3,1,2,0:T(4,128)(2,1)}), bf16[4,4,135,128]{3,1,2,0:T(4,128)(2,1)S(1)}, u32[]{:S(2)}, u32[]{:S(2)}) async-start(bf16[4,4,135,128]{3,1,2,0:T(4,128)(2,1)} %copy.55), calls=%async_computation | async-start | bytes 1105920 | tf_op jit(solution)/shard_map/all_to_all | solution.py:299
